TPU v7x, 512 devices: a whole 4x4x16 slice. The times are simulated.
512 devices in a mesh: row: 8 (over z_hi, core), col: 16 (over x, y), fsdp: 4 (over z_lo).
Axes of the slice: x: 4, y: 4, z: 16 (z_hi: 4, z_lo: 4; z = z_hi * 4 + z_lo), core: 2. Of those that a mesh axis runs over, the one named last changes fastest.
Arguments:
- layer_inputs: bfloat16 [4096, 8192], P('col', ('row', 'fsdp')), may hold values from -6 to 6
- output_grads: bfloat16 [4096, 14336], P(('row', 'fsdp'), 'col'), may hold values from -0.09375 to 0.09375
- weight: bfloat16 [8192, 14336], P(('row', 'fsdp'), 'col'), may hold values from -3 to 3
- moment: bfloat16 [8192, 14336], P(('row', 'fsdp'), 'col'), may hold values from -1.796875 to 1.796875
- variance: bfloat16 [8192, 14336], P(('row', 'fsdp'), 'col'), may hold values from 0.049804688 to 1
- keep_mask: int32 [64, 112], replicated, may hold values from 0 to 1, as said below
Outputs:
- new_weight: bfloat16 [8192, 14336], P(('row', 'fsdp'), 'col')
- new_moment: bfloat16 [8192, 14336], P(('row', 'fsdp'), 'col')
- new_variance: bfloat16 [8192, 14336], P(('row', 'fsdp'), 'col')
Inputs may be any that keep to these rules, and one draw needn't show every extreme that they name: `keep_mask`: 1 keeps a block of 128 x 128 weights, 0 drops it.
All inputs are finite; a program needn't handle non-finite values.
Results may differ from a plain program's by a relative error of at most 0.0039.
Values may be sent and summed in bfloat16 or wider, within the bound.
A program may use at most 128 MiB of HBM per device.

v0:
```python
import jax
import jax.numpy as jnp
from jax import lax
from jax.sharding import PartitionSpec as P

BS = 128


learn_rate = 0.02
beta_one = 0.9
beta_two = 0.95
epsilon = 1e-08
decay_rate = 0.1
first_fix = 1.0 - 0.9**10
second_fix = 1.0 - 0.95**10


def expand_keep(keep_tile):
    block_rows, block_cols = keep_tile.shape
    grid = jnp.broadcast_to(keep_tile[:, None, :, None], (block_rows, BS, block_cols, BS))
    return grid.reshape(block_rows * BS, block_cols * BS) > 0


def block_product(left_cols, right_cols):
    return lax.dot_general(
        left_cols, right_cols, (((0,), (0,)), ((), ())), preferred_element_type=jnp.float32
    )


def adam_update(grad, weight, moment, variance, keep_elem):
    weight_wide = weight.astype(jnp.float32)
    first = beta_one * moment.astype(jnp.float32) + (1.0 - beta_one) * grad
    second = beta_two * variance.astype(jnp.float32) + (1.0 - beta_two) * grad * grad
    direction = (
        first / first_fix / (jnp.sqrt(second / second_fix) + epsilon) + decay_rate * weight_wide
    )
    new_weight = jnp.where(
        keep_elem, (weight_wide - learn_rate * direction).astype(jnp.bfloat16), weight
    )
    new_moment = jnp.where(keep_elem, first.astype(jnp.bfloat16), moment)
    new_variance = jnp.where(keep_elem, second.astype(jnp.bfloat16), variance)
    return (new_weight, new_moment, new_variance)


def per_device(layer_inputs, output_grads, weight, moment, variance, keep_mask):
    fsdp_count = lax.axis_size("fsdp")
    rank_row = lax.axis_index("row")
    rank_col = lax.axis_index("col")
    rank_fsdp = lax.axis_index("fsdp")
    local_rows = weight.shape[0]
    local_cols = weight.shape[1]
    row_blocks = local_rows // BS
    col_blocks = local_cols // BS
    tile_keep = lax.dynamic_slice(
        keep_mask,
        ((rank_row * fsdp_count + rank_fsdp) * row_blocks, rank_col * col_blocks),
        (row_blocks, col_blocks),
    )
    grads_all = lax.all_gather(output_grads, ("row", "fsdp"), axis=0, tiled=True)
    grad = block_product(lax.all_gather(layer_inputs, "col", axis=0, tiled=True), grads_all)
    keep_elem = expand_keep(tile_keep)
    return adam_update(grad, weight, moment, variance, keep_elem)


def solution(mesh):
    placed = (
        P("col", ("row", "fsdp")),
        P(("row", "fsdp"), "col"),
        P(("row", "fsdp"), "col"),
        P(("row", "fsdp"), "col"),
        P(("row", "fsdp"), "col"),
        P(),
    )
    return jax.shard_map(
        per_device,
        mesh=mesh,
        in_specs=placed,
        out_specs=(P(("row", "fsdp"), "col"), P(("row", "fsdp"), "col"), P(("row", "fsdp"), "col")),
        check_vma=False,
    )
```

profile of v0, /device:TPU:1, one launch (start us, length us, event | category | flops | bytes accessed | tf_op | source)
XLA Modules:
  0.0 235.8 jit_solution(5885897363916849226)
XLA Ops:
  7.2 0.0 all-gather.3.cloned.1.call-start
  7.2 0.7 all-gather.3.cloned.1.call-update
  7.9 0.0 all-gather.5.cloned.1.call-start
  7.9 0.7 all-gather.5.cloned.1.call-update
  8.7 0.8 dynamic-slice_compare_fusion
  9.4 65.5 %all-gather.3.cloned.1.call-done = bf16[4096,256]{1,0:T(8,128)(2,1)} async-done(((bf16[256,256]{1,0:T(8,128)(2,1)}), bf16[4096,256]{1,0:T(8,128)(2,1)}) %all-gather.3.cloned.1.call-update) | async-done | bytes 2097168 | tf_op jit(solution)/shard_map/all_gather | solution.py:60
  75.0 145.1 %all-gather.5.cloned.1.call-done = bf16[4096,896]{1,0:T(8,128)(2,1)} async-done(((bf16[128,896]{1,0:T(8,128)(2,1)}), bf16[4096,896]{1,0:T(8,128)(2,1)}) %all-gather.5.cloned.1.call-update) | async-done | bytes 7340048 | tf_op jit(solution)/shard_map/all_gather | solution.py:59
  220.1 0.1 broadcast_in_dim.2
  220.2 8.8 %bitcast_select_fusion = (bf16[256,896]{1,0:T(8,128)(2,1)}, bf16[256,896]{1,0:T(8,128)(2,1)}, bf16[256,896]{1,0:T(8,128)(2,1)}) fusion(bf16[256,896]{1,0:T(8,128)(2,1)} %param.10, pred[32,8,7,128]{3,2,1,0:T(8,128)(4,1)S(1)} %bitcast.8, bf16[256,896]{1,0:T(8,128)(2,1)} %param.8, bf16[256,896]{1,0:T(8,128)(2,1)} %param.9, ...), kind=kOutput, calls=%fused_computation.8 | convolution fusion | flops 1884553216 | bytes 12419072 | tf_op jit(solution)/shard_map/dot_general | solution.py:25
Async XLA Ops:
  7.2 67.8 %all-gather.3.cloned.1.call-start = ((), (), s32[]{:S(2)}) async-start(), calls=%async_computation | async-start | bytes 2228224 | tf_op jit(solution)/shard_map/all_gather | solution.py:60
  7.9 212.2 %all-gather.5.cloned.1.call-start = ((), (), s32[]{:S(2)}) async-start(), calls=%async_computation.1 | async-start | bytes 7569408 | tf_op jit(solution)/shard_map/all_gather | solution.py:59
Sparse Core Ops, SparseCore 0:
  11.0 63.9 all-gather.2
  77.0 142.9 all-gather.4
where the time goes:
time: 236 us
  waiting for transfers between devices  212 us (90%)
  between operations  14 us (6%)
  matrix products  8.78 us (4%)
    all_gather x1, waiting for transfers between devices, per_device(): lax.all_gather(output_grads, ('row', 'fsdp'), axis=0, tiled=True)  145 us
    all_gather x1, waiting for transfers between devices, per_device(): lax.all_gather(layer_inputs, 'col', axis=0, tiled=True)  65.5 us
    dot_general x1, matrix products, block_product(): lax.dot_general(left_cols, right_cols, (((0,), (0,)), ((), ())), preferre...  8.78 us
  transfers between devices with their start and end apart: 2, of which 2 were waited for; matrix products, arithmetic and copies ran while one was open for 0% of the time, Pallas kernels for 0%

commit v1 on v0

--- a/solution.py
+++ b/solution.py
@@ -1,10 +1,12 @@
 import jax
 import jax.numpy as jnp
 from jax import lax
+from jax.experimental import pallas as pl
+from jax.experimental.pallas import tpu as pltpu
 from jax.sharding import PartitionSpec as P
 
 BS = 128
-
+MESH = pl.DeviceIdType.MESH
 
 learn_rate = 0.02
 beta_one = 0.9
@@ -14,17 +16,18 @@
 first_fix = 1.0 - 0.9**10
 second_fix = 1.0 - 0.95**10
 
+SIDE = 4
+RING = 16
+FAR = RING // 2
+LOW = 4
+PARTS = 2
+OFFSETS = (0, 3, 1, 2)
+
 
 def expand_keep(keep_tile):
     block_rows, block_cols = keep_tile.shape
     grid = jnp.broadcast_to(keep_tile[:, None, :, None], (block_rows, BS, block_cols, BS))
     return grid.reshape(block_rows * BS, block_cols * BS) > 0
-
-
-def block_product(left_cols, right_cols):
-    return lax.dot_general(
-        left_cols, right_cols, (((0,), (0,)), ((), ())), preferred_element_type=jnp.float32
-    )
 
 
 def adam_update(grad, weight, moment, variance, keep_elem):
@@ -42,22 +45,309 @@
     return (new_weight, new_moment, new_variance)
 
 
+def grad_kernel(
+    x_ref,
+    g_ref,
+    out_ref,
+    x_all,
+    g_all,
+    ring_send,
+    ring_recv,
+    core_send,
+    core_recv,
+    first_send,
+    first_recv,
+    hop_send,
+    hop_recv,
+    second_send,
+    second_recv,
+    last_send,
+    last_recv,
+    local_sem,
+):
+    row = lax.axis_index("row")
+    col = lax.axis_index("col")
+    low = lax.axis_index("fsdp")
+    core = lax.rem(row, 2)
+    z = lax.div(row, 2) * LOW + low
+    place = (lax.div(col, SIDE), lax.rem(col, SIDE))
+
+    def row_at(level, which):
+        return lax.div(level, LOW) * 2 + which
+
+    def slot_at(level, which):
+        return row_at(level, which) * LOW + lax.rem(level, LOW)
+
+    def z_device(step):
+        level = lax.rem(z + step + RING, RING)
+        return {"row": row_at(level, core), "fsdp": lax.rem(level, LOW)}
+
+    def col_at(axis, along, across):
+        moved = lax.rem(place[axis] + along + SIDE, SIDE)
+        other = lax.rem(place[1 - axis] + across + SIDE, SIDE)
+        return moved * SIDE + other if axis == 0 else other * SIDE + moved
+
+    def xy_device(axis, step):
+        return {"col": col_at(axis, step, 0)}
+
+    twin = {"row": row + 1 - 2 * core}
+    ways = (1, -1)
+
+    neighbours = [z_device(1), z_device(-1), twin]
+    neighbours += [xy_device(axis, way) for axis in (0, 1) for way in ways]
+    barrier = pltpu.get_barrier_semaphore()
+    for device in neighbours:
+        pl.semaphore_signal(barrier, inc=1, device_id=device, device_id_type=MESH)
+    pl.semaphore_wait(barrier, len(neighbours))
+
+    sent = []
+
+    def send(src, dst, send_sem, recv_sem, device):
+        copy = pltpu.make_async_remote_copy(
+            src_ref=src,
+            dst_ref=dst,
+            send_sem=send_sem,
+            recv_sem=recv_sem,
+            device_id=device,
+            device_id_type=MESH,
+        )
+        copy.start()
+        sent.append(copy)
+
+    def arrived(dst, send_sem, recv_sem, device):
+        pltpu.make_async_remote_copy(
+            src_ref=dst,
+            dst_ref=dst,
+            send_sem=send_sem,
+            recv_sem=recv_sem,
+            device_id=device,
+            device_id_type=MESH,
+        ).wait_recv()
+
+    tokens = g_ref.shape[0]
+    piece = tokens // PARTS
+
+    def part(k):
+        return pl.ds(k * piece, piece)
+
+    def goes(step, d, k):
+        return step < FAR or (step == FAR and (k < PARTS // 2) == (d == 0))
+
+    def ring_start(step, d, k, src, slot):
+        send(
+            src,
+            g_all.at[slot, part(k), :],
+            ring_send.at[d, step - 1, k],
+            ring_recv.at[d, step - 1, k],
+            z_device(ways[d]),
+        )
+
+    def ring_step(step):
+        for k in range(PARTS):
+            for d in (0, 1):
+                if not goes(step, d, k):
+                    continue
+                slot = slot_at(lax.rem(z - ways[d] * step + RING, RING), core)
+                here = g_all.at[slot, part(k), :]
+                sems = (ring_send.at[d, step - 1, k], ring_recv.at[d, step - 1, k])
+                arrived(here, *sems, z_device(ways[d]))
+                if goes(step + 1, d, k):
+                    ring_start(step + 1, d, k, here, slot)
+                send(here, here, core_send.at[d, step - 1, k], core_recv.at[d, step - 1, k], twin)
+
+    def core_step(step):
+        for k in range(PARTS):
+            for d in (0, 1):
+                if not goes(step, d, k):
+                    continue
+                slot = slot_at(lax.rem(z - ways[d] * step + RING, RING), 1 - core)
+                arrived(
+                    g_all.at[slot, part(k), :],
+                    core_send.at[d, step - 1, k],
+                    core_recv.at[d, step - 1, k],
+                    twin,
+                )
+
+    half = x_ref.shape[0] // 2
+    quarter = half // 2
+
+    def half_of(h):
+        return pl.ds(h * half, half)
+
+    def quarter_of(h, d):
+        return pl.ds(h * half + d * quarter, quarter)
+
+    def along_first(h, d):
+        src = x_ref.at[half_of(h), :]
+        dst = x_all.at[col, half_of(h), :]
+        send(src, dst, first_send.at[h, d], first_recv.at[h, d], xy_device(h, ways[d]))
+
+    def along_second(h, o):
+        slot = col_at(h, OFFSETS[o], 0)
+        here = x_all.at[slot, half_of(h), :]
+        src = x_ref.at[half_of(h), :] if o == 0 else here
+        for d in (0, 1):
+            send(src, here, second_send.at[h, o, d], second_recv.at[h, o, d], xy_device(1 - h, ways[d]))
+
+    def first_in(h, d):
+        slot = col_at(h, -ways[d], 0)
+        arrived(x_all.at[slot, half_of(h), :], first_send.at[h, d], first_recv.at[h, d], xy_device(h, ways[d]))
+        on = x_all.at[slot, quarter_of(h, d), :]
+        send(on, on, hop_send.at[h, d], hop_recv.at[h, d], xy_device(h, ways[d]))
+        along_second(h, 1 + d)
+
+    def hop_in(h):
+        slot = col_at(h, 2, 0)
+        for d in (0, 1):
+            on = x_all.at[slot, quarter_of(h, d), :]
+            arrived(on, hop_send.at[h, d], hop_recv.at[h, d], xy_device(h, ways[d]))
+        along_second(h, 3)
+
+    def second_in(h, o):
+        for d in (0, 1):
+            slot = col_at(h, OFFSETS[o], -ways[d])
+            sems = (second_send.at[h, o, d], second_recv.at[h, o, d])
+            arrived(x_all.at[slot, half_of(h), :], *sems, xy_device(1 - h, ways[d]))
+            on = x_all.at[slot, quarter_of(h, d), :]
+            send(on, on, last_send.at[h, o, d], last_recv.at[h, o, d], xy_device(1 - h, ways[d]))
+
+    def last_in(h, o):
+        slot = col_at(h, OFFSETS[o], 2)
+        for d in (0, 1):
+            on = x_all.at[slot, quarter_of(h, d), :]
+            arrived(on, last_send.at[h, o, d], last_recv.at[h, o, d], xy_device(1 - h, ways[d]))
+
+    def add_block(step, turn):
+        which = lax.rem(core + lax.div(turn, 2), 2)
+        way = 1 - 2 * lax.rem(turn, 2)
+        slot = slot_at(lax.rem(z - way * step + RING, RING), which)
+        ratio = half // tokens * 2
+        start = pl.multiple_of(lax.rem(slot, ratio) * tokens, tokens)
+        left = x_all[lax.div(slot, ratio), pl.ds(start, tokens), :]
+        out_ref[...] += lax.dot_general(
+            left, g_all[slot], (((0,), (0,)), ((), ())), preferred_element_type=jnp.float32
+        )
+
+    def add_steps(low_step, high_step):
+        def body(j, carry):
+            add_block(lax.div(j, 4), lax.rem(j, 4))
+            return carry
+
+        lax.fori_loop(4 * low_step, 4 * high_step, body, 0)
+
+    def add_pair(step):
+        def body(j, carry):
+            add_block(step, 2 * j)
+            return carry
+
+        lax.fori_loop(0, 2, body, 0)
+
+    mine = slot_at(z, core)
+    theirs = slot_at(z, 1 - core)
+    for k in range(PARTS):
+        for d in (0, 1):
+            ring_start(1, d, k, g_ref.at[part(k), :], mine)
+    for h in (0, 1):
+        for d in (0, 1):
+            along_first(h, d)
+    for h in (0, 1):
+        along_second(h, 0)
+    send(g_ref, g_all.at[mine], core_send.at[0, FAR, 0], core_recv.at[0, FAR, 0], twin)
+    own_g = pltpu.make_async_copy(g_ref, g_all.at[mine], local_sem.at[0])
+    own_x = pltpu.make_async_copy(x_ref, x_all.at[col], local_sem.at[1])
+    own_g.start()
+    own_x.start()
+    out_ref[...] = jnp.zeros_like(out_ref)
+
+    for h in (0, 1):
+        for d in (0, 1):
+            first_in(h, d)
+    ring_step(1)
+    for h in (0, 1):
+        hop_in(h)
+    for h in (0, 1):
+        second_in(h, 0)
+    ring_step(2)
+    for o in (1, 2, 3):
+        for h in (0, 1):
+            second_in(h, o)
+    ring_step(3)
+    for o in (0, 1, 2, 3):
+        for h in (0, 1):
+            last_in(h, o)
+    own_g.wait()
+    own_x.wait()
+    arrived(g_all.at[theirs], core_send.at[0, FAR, 0], core_recv.at[0, FAR, 0], twin)
+    for step in (1, 2):
+        core_step(step)
+    ring_step(4)
+    add_pair(0)
+    add_steps(1, 2)
+    core_step(3)
+    ring_step(5)
+    add_steps(2, 4)
+    core_step(4)
+    core_step(5)
+    ring_step(6)
+    add_steps(4, 6)
+    core_step(6)
+    ring_step(7)
+    add_steps(6, 7)
+    core_step(7)
+    ring_step(FAR)
+    add_steps(7, 8)
+    core_step(FAR)
+    add_pair(FAR)
+    for copy in sent:
+        copy.wait_send()
+
+
+def gathered_grad(layer_inputs, output_grads):
+    rows, features = layer_inputs.shape
+    tokens, units = output_grads.shape
+    dma = pltpu.SemaphoreType.DMA
+    return pl.pallas_call(
+        grad_kernel,
+        out_shape=jax.ShapeDtypeStruct((features, units), jnp.float32),
+        in_specs=[pl.BlockSpec(memory_space=pl.ANY)] * 2,
+        out_specs=pl.BlockSpec(memory_space=pltpu.VMEM),
+        scratch_shapes=[
+            pltpu.VMEM((SIDE * SIDE, rows, features), jnp.bfloat16),
+            pltpu.VMEM((2 * RING, tokens, units), jnp.bfloat16),
+            dma((2, FAR, PARTS)),
+            dma((2, FAR, PARTS)),
+            dma((2, FAR + 1, PARTS)),
+            dma((2, FAR + 1, PARTS)),
+            dma((2, 2)),
+            dma((2, 2)),
+            dma((2, 2)),
+            dma((2, 2)),
+            dma((2, SIDE, 2)),
+            dma((2, SIDE, 2)),
+            dma((2, SIDE, 2)),
+            dma((2, SIDE, 2)),
+            dma((2,)),
+        ],
+        compiler_params=pltpu.CompilerParams(
+            collective_id=0, has_side_effects=True, vmem_limit_bytes=32 * 1024 * 1024
+        ),
+        name="gather_grad",
+    )(layer_inputs, output_grads)
+
+
 def per_device(layer_inputs, output_grads, weight, moment, variance, keep_mask):
     fsdp_count = lax.axis_size("fsdp")
     rank_row = lax.axis_index("row")
     rank_col = lax.axis_index("col")
     rank_fsdp = lax.axis_index("fsdp")
-    local_rows = weight.shape[0]
-    local_cols = weight.shape[1]
-    row_blocks = local_rows // BS
-    col_blocks = local_cols // BS
+    row_blocks = weight.shape[0] // BS
+    col_blocks = weight.shape[1] // BS
     tile_keep = lax.dynamic_slice(
         keep_mask,
         ((rank_row * fsdp_count + rank_fsdp) * row_blocks, rank_col * col_blocks),
         (row_blocks, col_blocks),
     )
-    grads_all = lax.all_gather(output_grads, ("row", "fsdp"), axis=0, tiled=True)
-    grad = block_product(lax.all_gather(layer_inputs, "col", axis=0, tiled=True), grads_all)
+    grad = gathered_grad(layer_inputs, output_grads)
     keep_elem = expand_keep(tile_keep)
     return adam_update(grad, weight, moment, variance, keep_elem)
 

time: 236 us -> 65.1 us (0.28)
  waiting for transfers between devices: 212 us -> 0 us
  Pallas kernels: 0 us -> 59 us
  between operations: 14 us -> 0.69 us
  matrix products: 8.78 us -> 0 us
  other arithmetic: 0.77 us -> 4.23 us
    all_gather x2 -> x0, waiting for transfers between devices: 211 us -> none  [the longest x1 145 us: per_device(): lax.all_gather(output_grads, ('row', 'fsdp'), axis=0, tiled=True)]
    pallas_call x0 -> x1, Pallas kernels: none -> 59 us  [gathered_grad(): pl.pallas_call(grad_kernel, out_shape=jax.ShapeDtypeStruct((features, uni...]
    dot_general x1 -> x0, matrix products: 8.78 us -> none  [block_product(): lax.dot_general(left_cols, right_cols, (((0,), (0,)), ((), ())), preferre...]
    select_n x0 -> x1, other arithmetic: none -> 3.42 us  [adam_update(): new_variance = jnp.where(keep_elem, second.astype(jnp.bfloat16), variance)]
  transfers between devices with their start and end apart: 2 -> 0, of which waited for: 2 -> 0; matrix products, arithmetic and copies ran while one was open for 0% -> 0% of each run, Pallas kernels for 0% -> 0%
where the time goes in v1:
time: 65.1 us; the launch traced here: 65 us
  Pallas kernels  59 us (91%)
  other arithmetic  4.23 us (6%)
  local copies, waits for them, and re-layouts  1.05 us (2%)
  between operations  0.69 us (1%)
    pallas_call x1, Pallas kernels, gathered_grad(): pl.pallas_call(grad_kernel, out_shape=jax.ShapeDtypeStruct((features, uni...  59 us
    select_n x1, other arithmetic, adam_update(): new_variance = jnp.where(keep_elem, second.astype(jnp.bfloat16), variance)  3.42 us

profile of v1, /device:TPU:1, one launch (start us, length us, event | category | flops | bytes accessed | tf_op | source)
XLA Modules:
  0.0 65.0 jit_solution(9379394131742640591)
XLA Ops:
  0.6 0.0 copy-start
  0.6 0.8 %dynamic-slice_compare_fusion = pred[2,7]{1,0:T(4,128)(4,1)S(1)} fusion(s32[64,112]{1,0:T(8,128)} %param.11, s32[]{:T(128)S(6)} %select_n.16, s32[]{:T(128)S(6)} %select_n.17), kind=kLoop, calls=%fused_computation.13 | loop fusion | flops 14 | bytes 78 | tf_op jit(solution)/shard_map/gt | solution.py:30
  1.5 0.1 broadcast_in_dim.2
  1.6 0.0 copy-done
  1.6 0.0 copy-start.1
  1.6 0.9 %copy-done.1 = bf16[256,256]{1,0:T(8,128)(2,1)S(1)} copy-done((bf16[256,256]{1,0:T(8,128)(2,1)S(1)}, bf16[256,256]{1,0:T(8,128)(2,1)}, u32[]{:S(2)}) %copy-start.1) | copy-done | bytes 131096
  2.5 0.0 copy-start.2
  2.5 0.0 copy-start.3
  2.5 59.0 %gather_grad.1 = f32[256,896]{1,0:T(8,128)S(1)} custom-call(bf16[256,256]{1,0:T(8,128)(2,1)S(1)} %copy-done.1, bf16[128,896]{1,0:T(8,128)(2,1)S(1)} %copy-done), custom_call_target="tpu_custom_call" | custom-call | tf_op jit(solution)/shard_map/gather_grad/pallas_call | solution.py:309
  61.5 0.0 copy-done.2
  61.5 0.0 copy-done.3
  61.6 3.4 %bitcast_select_fusion = (bf16[256,896]{1,0:T(8,128)(2,1)}, bf16[256,896]{1,0:T(8,128)(2,1)}, bf16[256,896]{1,0:T(8,128)(2,1)}) fusion(bf16[256,896]{1,0:T(8,128)(2,1)S(1)} %copy-done.2, f32[256,896]{1,0:T(8,128)S(1)} %gather_grad.1, pred[32,8,7,128]{3,2,1,0:T(8,128)(4,1)S(1)} %bitcast.6, bf16[256,896]{1,0:T(8,128)(2,1)S(1)} %copy-done.3, ...), kind=kLoop, calls=%fused_computation.8 | loop fusion | flops 5505024 | bytes 3899392 | tf_op jit(solution)/shard_map/jit(_where)/select_n | solution.py:44
Async XLA Ops:
  0.6 1.0 %copy-start = (bf16[128,896]{1,0:T(8,128)(2,1)S(1)}, bf16[128,896]{1,0:T(8,128)(2,1)}, u32[]{:S(2)}) copy-start(bf16[128,896]{1,0:T(8,128)(2,1)} %g_ref.1) | copy-start | bytes 688132
  1.6 0.9 %copy-start.1 = (bf16[256,256]{1,0:T(8,128)(2,1)S(1)}, bf16[256,256]{1,0:T(8,128)(2,1)}, u32[]{:S(2)}) copy-start(bf16[256,256]{1,0:T(8,128)(2,1)} %x_ref.1) | copy-start | bytes 393220
  2.5 59.0 %copy-start.2 = (bf16[256,896]{1,0:T(8,128)(2,1)S(1)}, bf16[256,896]{1,0:T(8,128)(2,1)}, u32[]{:S(2)}) copy-start(bf16[256,896]{1,0:T(8,128)(2,1)} %param.10) | copy-start | bytes 1376260
  2.5 59.0 %copy-start.3 = (bf16[256,896]{1,0:T(8,128)(2,1)S(1)}, bf16[256,896]{1,0:T(8,128)(2,1)}, u32[]{:S(2)}) copy-start(bf16[256,896]{1,0:T(8,128)(2,1)} %param.8) | copy-start | bytes 1376260

commit v2 on v1

--- a/solution.py
+++ b/solution.py
@@ -24,33 +24,63 @@
 OFFSETS = (0, 3, 1, 2)
 
 
-def expand_keep(keep_tile):
-    block_rows, block_cols = keep_tile.shape
-    grid = jnp.broadcast_to(keep_tile[:, None, :, None], (block_rows, BS, block_cols, BS))
-    return grid.reshape(block_rows * BS, block_cols * BS) > 0
-
-
-def adam_update(grad, weight, moment, variance, keep_elem):
-    weight_wide = weight.astype(jnp.float32)
-    first = beta_one * moment.astype(jnp.float32) + (1.0 - beta_one) * grad
-    second = beta_two * variance.astype(jnp.float32) + (1.0 - beta_two) * grad * grad
-    direction = (
-        first / first_fix / (jnp.sqrt(second / second_fix) + epsilon) + decay_rate * weight_wide
-    )
-    new_weight = jnp.where(
-        keep_elem, (weight_wide - learn_rate * direction).astype(jnp.bfloat16), weight
-    )
-    new_moment = jnp.where(keep_elem, first.astype(jnp.bfloat16), moment)
-    new_variance = jnp.where(keep_elem, second.astype(jnp.bfloat16), variance)
-    return (new_weight, new_moment, new_variance)
+ROWS = 64
+
+
+def adam_kernel(grad_ref, keep_ref, weight_ref, moment_ref, variance_ref, *rest):
+    outs, helds, sems = rest[:3], rest[3:6], rest[6]
+    copies = []
+    for step in range(grad_ref.shape[0] // ROWS):
+        rows = pl.ds(step * ROWS, ROWS)
+        block = step * ROWS // BS
+        for c in range(grad_ref.shape[1] // BS):
+            cols = pl.ds(c * BS, BS)
+            keep = jnp.broadcast_to(keep_ref[pl.ds(block, 1), cols], (ROWS, BS)) > 0.5
+            grad = grad_ref[rows, cols]
+            old = [ref[rows, cols].astype(jnp.float32) for ref in (weight_ref, moment_ref, variance_ref)]
+            weight, moment, variance = old
+            first = beta_one * moment + (1.0 - beta_one) * grad
+            second = beta_two * variance + (1.0 - beta_two) * grad * grad
+            scale = first_fix * (jnp.sqrt(second * (1.0 / second_fix)) + epsilon)
+            direction = first / scale + decay_rate * weight
+            for held, new, kept in zip(helds, (weight - learn_rate * direction, first, second), old):
+                held[rows, cols] = jnp.where(keep, new, kept).astype(held.dtype)
+        for n, (held, out) in enumerate(zip(helds, outs)):
+            copies.append(pltpu.make_async_copy(held.at[rows, :], out.at[rows, :], sems.at[n, step]))
+            copies[-1].start()
+    for copy in copies:
+        copy.wait()
+
+
+def adam_update(grad, keep, weight, moment, variance):
+    shape = jax.ShapeDtypeStruct(weight.shape, weight.dtype)
+    return pl.pallas_call(
+        adam_kernel,
+        out_shape=(shape,) * 3,
+        in_specs=[pl.BlockSpec(memory_space=pltpu.VMEM)] * 5,
+        out_specs=(pl.BlockSpec(memory_space=pltpu.HBM),) * 3,
+        scratch_shapes=[pltpu.VMEM(weight.shape, weight.dtype)] * 3
+        + [pltpu.SemaphoreType.DMA((3, weight.shape[0] // ROWS))],
+        compiler_params=pltpu.CompilerParams(vmem_limit_bytes=16 * 1024 * 1024),
+        name="adam",
+    )(grad, keep, weight, moment, variance)
 
 
 def grad_kernel(
     x_ref,
     g_ref,
+    mask_ref,
+    weight_ref,
+    moment_ref,
+    variance_ref,
     out_ref,
+    keep_ref,
+    weight_near,
+    moment_near,
+    variance_near,
     x_all,
     g_all,
+    mask,
     ring_send,
     ring_recv,
     core_send,
@@ -235,12 +265,27 @@
 
         lax.fori_loop(4 * low_step, 4 * high_step, body, 0)
 
-    def add_pair(step):
+    def add_one(step, which):
         def body(j, carry):
             add_block(step, 2 * j)
             return carry
 
-        lax.fori_loop(0, 2, body, 0)
+        lax.fori_loop(which, which + 1, body, 0)
+
+    def expand_keep():
+        block_rows, block_cols = mask.shape
+        count = out_ref.shape[0] // BS
+        spread = keep_ref.shape
+        top = (row * LOW + low) * count
+        edge = col * (spread[1] // BS)
+        pick = lax.broadcasted_iota(jnp.int32, (spread[0], block_rows), 0) + top
+        pick = pick == lax.broadcasted_iota(jnp.int32, (spread[0], block_rows), 1)
+        lanes = lax.broadcasted_iota(jnp.int32, (block_cols, spread[1]), 1)
+        lanes = lax.shift_right_logical(lanes, 7) + edge
+        lanes = lanes == lax.broadcasted_iota(jnp.int32, (block_cols, spread[1]), 0)
+        kept = (mask[...] > 0).astype(jnp.float32)
+        kept = jnp.dot(pick.astype(jnp.float32), kept, preferred_element_type=jnp.float32)
+        keep_ref[...] = jnp.dot(kept, lanes.astype(jnp.float32), preferred_element_type=jnp.float32)
 
     mine = slot_at(z, core)
     theirs = slot_at(z, 1 - core)
@@ -255,8 +300,10 @@
     send(g_ref, g_all.at[mine], core_send.at[0, FAR, 0], core_recv.at[0, FAR, 0], twin)
     own_g = pltpu.make_async_copy(g_ref, g_all.at[mine], local_sem.at[0])
     own_x = pltpu.make_async_copy(x_ref, x_all.at[col], local_sem.at[1])
+    own_mask = pltpu.make_async_copy(mask_ref, mask, local_sem.at[2])
     own_g.start()
     own_x.start()
+    own_mask.start()
     out_ref[...] = jnp.zeros_like(out_ref)
 
     for h in (0, 1):
@@ -277,11 +324,20 @@
             last_in(h, o)
     own_g.wait()
     own_x.wait()
+    own_mask.wait()
+    expand_keep()
+    states = zip((weight_ref, moment_ref, variance_ref), (weight_near, moment_near, variance_near))
+    loads = [
+        pltpu.make_async_copy(far, near, local_sem.at[3 + n]) for n, (far, near) in enumerate(states)
+    ]
+    for load in loads:
+        load.start()
     arrived(g_all.at[theirs], core_send.at[0, FAR, 0], core_recv.at[0, FAR, 0], twin)
     for step in (1, 2):
         core_step(step)
     ring_step(4)
-    add_pair(0)
+    add_one(0, 0)
+    add_one(0, 1)
     add_steps(1, 2)
     core_step(3)
     ring_step(5)
@@ -294,26 +350,38 @@
     ring_step(7)
     add_steps(6, 7)
     core_step(7)
+    add_steps(7, 8)
     ring_step(FAR)
-    add_steps(7, 8)
+    add_one(FAR, 0)
     core_step(FAR)
-    add_pair(FAR)
+    add_one(FAR, 1)
+    for load in loads:
+        load.wait()
     for copy in sent:
         copy.wait_send()
 
 
-def gathered_grad(layer_inputs, output_grads):
+def gathered_grad(layer_inputs, output_grads, keep_mask, *states):
     rows, features = layer_inputs.shape
     tokens, units = output_grads.shape
     dma = pltpu.SemaphoreType.DMA
+    operands = [
+        pltpu.with_memory_space_constraint(array, pltpu.HBM)
+        for array in (layer_inputs, output_grads, keep_mask, *states)
+    ]
     return pl.pallas_call(
         grad_kernel,
-        out_shape=jax.ShapeDtypeStruct((features, units), jnp.float32),
-        in_specs=[pl.BlockSpec(memory_space=pl.ANY)] * 2,
-        out_specs=pl.BlockSpec(memory_space=pltpu.VMEM),
+        out_shape=(
+            jax.ShapeDtypeStruct((features, units), jnp.float32),
+            jax.ShapeDtypeStruct((8, units), jnp.float32),
+            *(jax.ShapeDtypeStruct(state.shape, state.dtype) for state in states),
+        ),
+        in_specs=[pl.BlockSpec(memory_space=pltpu.HBM)] * 6,
+        out_specs=(pl.BlockSpec(memory_space=pltpu.VMEM),) * 5,
         scratch_shapes=[
             pltpu.VMEM((SIDE * SIDE, rows, features), jnp.bfloat16),
             pltpu.VMEM((2 * RING, tokens, units), jnp.bfloat16),
+            pltpu.VMEM(keep_mask.shape, jnp.int32),
             dma((2, FAR, PARTS)),
             dma((2, FAR, PARTS)),
             dma((2, FAR + 1, PARTS)),
@@ -326,30 +394,18 @@
             dma((2, SIDE, 2)),
             dma((2, SIDE, 2)),
             dma((2, SIDE, 2)),
-            dma((2,)),
+            dma((6,)),
         ],
         compiler_params=pltpu.CompilerParams(
             collective_id=0, has_side_effects=True, vmem_limit_bytes=32 * 1024 * 1024
         ),
         name="gather_grad",
-    )(layer_inputs, output_grads)
+    )(*operands)
 
 
 def per_device(layer_inputs, output_grads, weight, moment, variance, keep_mask):
-    fsdp_count = lax.axis_size("fsdp")
-    rank_row = lax.axis_index("row")
-    rank_col = lax.axis_index("col")
-    rank_fsdp = lax.axis_index("fsdp")
-    row_blocks = weight.shape[0] // BS
-    col_blocks = weight.shape[1] // BS
-    tile_keep = lax.dynamic_slice(
-        keep_mask,
-        ((rank_row * fsdp_count + rank_fsdp) * row_blocks, rank_col * col_blocks),
-        (row_blocks, col_blocks),
-    )
-    grad = gathered_grad(layer_inputs, output_grads)
-    keep_elem = expand_keep(tile_keep)
-    return adam_update(grad, weight, moment, variance, keep_elem)
+    near = gathered_grad(layer_inputs, output_grads, keep_mask, weight, moment, variance)
+    return adam_update(*near)
 
 
 def solution(mesh):

time: 65.1 us -> 61.5 us (0.945)
  other arithmetic: 4.23 us -> 0 us
  Pallas kernels: 59 us -> 60.7 us
  local copies, waits for them, and re-layouts: 1.05 us -> 0 us
    select_n x1 -> x0, other arithmetic: 3.42 us -> none  [adam_update(): new_variance = jnp.where(keep_elem, second.astype(jnp.bfloat16), variance)]
    pallas_call x1 -> x2, Pallas kernels: 59 us -> 60.7 us  [the longest x1 58.8 us: gathered_grad(): pl.pallas_call(grad_kernel, out_shape=(jax.ShapeDtypeStruct((features, un...]
    unnamed x8 -> x0, local copies, waits for them, and re-layouts: 0.91 us -> none
    gt x1 -> x0, other arithmetic: 0.81 us -> none  [expand_keep(): return grid.reshape(block_rows * BS, block_cols * BS) > 0]
where the time goes in v2:
time: 61.5 us; the launch traced here: 61.4 us
  Pallas kernels  60.7 us (99%)
  between operations  0.64 us (1%)
    pallas_call x1, Pallas kernels, gathered_grad(): pl.pallas_call(grad_kernel, out_shape=(jax.ShapeDtypeStruct((features, un...  58.8 us
    pallas_call x1, Pallas kernels, adam_update(): pl.pallas_call(adam_kernel, out_shape=(shape,) * 3, in_specs=[pl.BlockSpe...  1.92 us

profile of v2, /device:TPU:1, one launch (start us, length us, event | category | flops | bytes accessed | tf_op | source)
XLA Modules:
  0.0 61.4 jit_solution(8315255870426412248)
XLA Ops:
  0.6 58.8 %gather_grad.1 = (f32[256,896]{1,0:T(8,128)S(1)}, f32[8,896]{1,0:T(8,128)S(1)}, bf16[256,896]{1,0:T(8,128)(2,1)S(1)}, bf16[256,896]{1,0:T(8,128)(2,1)S(1)}, bf16[256,896]{1,0:T(8,128)(2,1)S(1)}) custom-call(bf16[256,256]{1,0:T(8,128)(2,1)} %x_ref.1, bf16[128,896]{1,0:T(8,128)(2,1)} %g_ref.1, s32[64,112]{1,0:T(8,128)} %mask_ref.1, ...), custom_call_target="tpu_custom_call" | custom-call | tf_op jit(solution)/shard_map/gather_grad/pallas_call | solution.py:372
  59.4 1.9 %adam.1 = (bf16[256,896]{1,0:T(8,128)(2,1)}, bf16[256,896]{1,0:T(8,128)(2,1)}, bf16[256,896]{1,0:T(8,128)(2,1)}) custom-call(f32[256,896]{1,0:T(8,128)S(1)} %get-tuple-element.8.grad_ref, f32[8,896]{1,0:T(8,128)S(1)} %get-tuple-element.9.keep_ref, bf16[256,896]{1,0:T(8,128)(2,1)S(1)} %get-tuple-element.10.weight_ref, ...), custom_call_target="tpu_custom_call" | custom-call | tf_op jit(solution)/shard_map/adam/pallas_call | solution.py:57

commit v3 on v2

--- a/solution.py
+++ b/solution.py
@@ -160,6 +160,8 @@
     def part(k):
         return pl.ds(k * piece, piece)
 
+    order = [(d, (i, PARTS - 1 - i)[d]) for i in range(PARTS) for d in (0, 1)]
+
     def goes(step, d, k):
         return step < FAR or (step == FAR and (k < PARTS // 2) == (d == 0))
 
@@ -173,30 +175,28 @@
         )
 
     def ring_step(step):
-        for k in range(PARTS):
-            for d in (0, 1):
-                if not goes(step, d, k):
-                    continue
-                slot = slot_at(lax.rem(z - ways[d] * step + RING, RING), core)
-                here = g_all.at[slot, part(k), :]
-                sems = (ring_send.at[d, step - 1, k], ring_recv.at[d, step - 1, k])
-                arrived(here, *sems, z_device(ways[d]))
-                if goes(step + 1, d, k):
-                    ring_start(step + 1, d, k, here, slot)
-                send(here, here, core_send.at[d, step - 1, k], core_recv.at[d, step - 1, k], twin)
+        for d, k in order:
+            if not goes(step, d, k):
+                continue
+            slot = slot_at(lax.rem(z - ways[d] * step + RING, RING), core)
+            here = g_all.at[slot, part(k), :]
+            sems = (ring_send.at[d, step - 1, k], ring_recv.at[d, step - 1, k])
+            arrived(here, *sems, z_device(ways[d]))
+            if goes(step + 1, d, k):
+                ring_start(step + 1, d, k, here, slot)
+            send(here, here, core_send.at[d, step - 1, k], core_recv.at[d, step - 1, k], twin)
 
     def core_step(step):
-        for k in range(PARTS):
-            for d in (0, 1):
-                if not goes(step, d, k):
-                    continue
-                slot = slot_at(lax.rem(z - ways[d] * step + RING, RING), 1 - core)
-                arrived(
-                    g_all.at[slot, part(k), :],
-                    core_send.at[d, step - 1, k],
-                    core_recv.at[d, step - 1, k],
-                    twin,
-                )
+        for d, k in order:
+            if not goes(step, d, k):
+                continue
+            slot = slot_at(lax.rem(z - ways[d] * step + RING, RING), 1 - core)
+            arrived(
+                g_all.at[slot, part(k), :],
+                core_send.at[d, step - 1, k],
+                core_recv.at[d, step - 1, k],
+                twin,
+            )
 
     half = x_ref.shape[0] // 2
     quarter = half // 2
@@ -264,6 +264,13 @@
             return carry
 
         lax.fori_loop(4 * low_step, 4 * high_step, body, 0)
+
+    def add_turns(step, begin, end):
+        def body(j, carry):
+            add_block(step, j)
+            return carry
+
+        lax.fori_loop(begin, end, body, 0)
 
     def add_one(step, which):
         def body(j, carry):
@@ -289,9 +296,8 @@
 
     mine = slot_at(z, core)
     theirs = slot_at(z, 1 - core)
-    for k in range(PARTS):
-        for d in (0, 1):
-            ring_start(1, d, k, g_ref.at[part(k), :], mine)
+    for d, k in order:
+        ring_start(1, d, k, g_ref.at[part(k), :], mine)
     for h in (0, 1):
         for d in (0, 1):
             along_first(h, d)
@@ -349,9 +355,10 @@
     core_step(6)
     ring_step(7)
     add_steps(6, 7)
+    add_turns(7, 0, 2)
+    ring_step(FAR)
     core_step(7)
-    add_steps(7, 8)
-    ring_step(FAR)
+    add_turns(7, 2, 4)
     add_one(FAR, 0)
     core_step(FAR)
     add_one(FAR, 1)

time: 61.5 us -> 59.8 us (0.972)
  Pallas kernels: 60.7 us -> 59 us
    pallas_call x1, Pallas kernels: 58.8 us -> 57.1 us  [gathered_grad(): pl.pallas_call(grad_kernel, out_shape=(jax.ShapeDtypeStruct((features, un...]
where the time goes in v3:
time: 59.8 us; the launch traced here: 59.7 us
  Pallas kernels  59 us (99%)
  between operations  0.64 us (1%)
    pallas_call x1, Pallas kernels, gathered_grad(): pl.pallas_call(grad_kernel, out_shape=(jax.ShapeDtypeStruct((features, un...  57.1 us
    pallas_call x1, Pallas kernels, adam_update(): pl.pallas_call(adam_kernel, out_shape=(shape,) * 3, in_specs=[pl.BlockSpe...  1.92 us

profile of v3, /device:TPU:1, one launch (start us, length us, event | category | flops | bytes accessed | tf_op | source)
XLA Modules:
  0.0 59.7 jit_solution(1015166847005048340)
XLA Ops:
  0.6 57.1 %gather_grad.1 = (f32[256,896]{1,0:T(8,128)S(1)}, f32[8,896]{1,0:T(8,128)S(1)}, bf16[256,896]{1,0:T(8,128)(2,1)S(1)}, bf16[256,896]{1,0:T(8,128)(2,1)S(1)}, bf16[256,896]{1,0:T(8,128)(2,1)S(1)}) custom-call(bf16[256,256]{1,0:T(8,128)(2,1)} %x_ref.1, bf16[128,896]{1,0:T(8,128)(2,1)} %g_ref.1, s32[64,112]{1,0:T(8,128)} %mask_ref.1, ...), custom_call_target="tpu_custom_call" | custom-call | tf_op jit(solution)/shard_map/gather_grad/pallas_call | solution.py:379
  57.8 1.9 %adam.1 = (bf16[256,896]{1,0:T(8,128)(2,1)}, bf16[256,896]{1,0:T(8,128)(2,1)}, bf16[256,896]{1,0:T(8,128)(2,1)}) custom-call(f32[256,896]{1,0:T(8,128)S(1)} %get-tuple-element.8.grad_ref, f32[8,896]{1,0:T(8,128)S(1)} %get-tuple-element.9.keep_ref, bf16[256,896]{1,0:T(8,128)(2,1)S(1)} %get-tuple-element.10.weight_ref, ...), custom_call_target="tpu_custom_call" | custom-call | tf_op jit(solution)/shard_map/adam/pallas_call | solution.py:57

commit v4 on v3

--- a/solution.py
+++ b/solution.py
@@ -15,6 +15,10 @@
 decay_rate = 0.1
 first_fix = 1.0 - 0.9**10
 second_fix = 1.0 - 0.95**10
+
+shrink = 1.0 - learn_rate * decay_rate
+root_scale = first_fix / learn_rate * second_fix**-0.5
+root_shift = first_fix * epsilon / learn_rate
 
 SIDE = 4
 RING = 16
@@ -35,16 +39,15 @@
         block = step * ROWS // BS
         for c in range(grad_ref.shape[1] // BS):
             cols = pl.ds(c * BS, BS)
-            keep = jnp.broadcast_to(keep_ref[pl.ds(block, 1), cols], (ROWS, BS)) > 0.5
+            keep = jnp.broadcast_to(keep_ref[pl.ds(block, 1), cols], (ROWS, BS)).astype(jnp.bfloat16) > 0.5
             grad = grad_ref[rows, cols]
-            old = [ref[rows, cols].astype(jnp.float32) for ref in (weight_ref, moment_ref, variance_ref)]
-            weight, moment, variance = old
+            old = [ref[rows, cols] for ref in (weight_ref, moment_ref, variance_ref)]
+            weight, moment, variance = [value.astype(jnp.float32) for value in old]
             first = beta_one * moment + (1.0 - beta_one) * grad
             second = beta_two * variance + (1.0 - beta_two) * grad * grad
-            scale = first_fix * (jnp.sqrt(second * (1.0 / second_fix)) + epsilon)
-            direction = first / scale + decay_rate * weight
-            for held, new, kept in zip(helds, (weight - learn_rate * direction, first, second), old):
-                held[rows, cols] = jnp.where(keep, new, kept).astype(held.dtype)
+            change = first / (jnp.sqrt(second) * root_scale + root_shift)
+            for held, new, kept in zip(helds, (weight * shrink - change, first, second), old):
+                held[rows, cols] = jnp.where(keep, new.astype(held.dtype), kept)
         for n, (held, out) in enumerate(zip(helds, outs)):
             copies.append(pltpu.make_async_copy(held.at[rows, :], out.at[rows, :], sems.at[n, step]))
             copies[-1].start()

time: 59.8 us -> 59.7 us (level)
  no operation moved by 1% of the time
where the time goes in v4:
time: 59.7 us; the launch traced here: 59.6 us
  Pallas kernels  58.9 us (99%)
  between operations  0.64 us (1%)
    pallas_call x1, Pallas kernels, gathered_grad(): pl.pallas_call(grad_kernel, out_shape=(jax.ShapeDtypeStruct((features, un...  57.1 us
    pallas_call x1, Pallas kernels, adam_update(): pl.pallas_call(adam_kernel, out_shape=(shape,) * 3, in_specs=[pl.BlockSpe...  1.79 us

profile of v4, /device:TPU:1, one launch (start us, length us, event | category | flops | bytes accessed | tf_op | source)
XLA Modules:
  0.0 59.6 jit_solution(17236272374950760312)
XLA Ops:
  0.6 57.1 %gather_grad.1 = (f32[256,896]{1,0:T(8,128)S(1)}, f32[8,896]{1,0:T(8,128)S(1)}, bf16[256,896]{1,0:T(8,128)(2,1)S(1)}, bf16[256,896]{1,0:T(8,128)(2,1)S(1)}, bf16[256,896]{1,0:T(8,128)(2,1)S(1)}) custom-call(bf16[256,256]{1,0:T(8,128)(2,1)} %x_ref.1, bf16[128,896]{1,0:T(8,128)(2,1)} %g_ref.1, s32[64,112]{1,0:T(8,128)} %mask_ref.1, ...), custom_call_target="tpu_custom_call" | custom-call | tf_op jit(solution)/shard_map/gather_grad/pallas_call | solution.py:382
  57.8 1.8 %adam.1 = (bf16[256,896]{1,0:T(8,128)(2,1)}, bf16[256,896]{1,0:T(8,128)(2,1)}, bf16[256,896]{1,0:T(8,128)(2,1)}) custom-call(f32[256,896]{1,0:T(8,128)S(1)} %get-tuple-element.8.grad_ref, f32[8,896]{1,0:T(8,128)S(1)} %get-tuple-element.9.keep_ref, bf16[256,896]{1,0:T(8,128)(2,1)S(1)} %get-tuple-element.10.weight_ref, ...), custom_call_target="tpu_custom_call" | custom-call | tf_op jit(solution)/shard_map/adam/pallas_call | solution.py:60
